TPU v7x, 32 devices: a whole 2x2x4 slice. The times are simulated.
32 devices in a mesh: dp: 4 (over y, core), expert: 4 (over z), tensor: 2 (over x).
Axes of the slice: x: 2, y: 2, z: 4, core: 2. Of those that a mesh axis runs over, the one named last changes fastest.
Arguments:
- grad_out: bfloat16 [4096, 2048], P(('dp', 'expert', 'tensor')), may hold values from -6 to 6
- expert_ids: int32 [4096, 2], P(('dp', 'expert', 'tensor')), may hold values from 0 to 63, all different within a row; in each aligned block of 128 rows (0 to 127, 128 to 255, ...) at most 5 rows name the same one
- gate_weights: float32 [4096, 2], P(('dp', 'expert', 'tensor')), may hold values from 0.05 to 0.6
- overflow: int32 [4096, 2], P(('dp', 'expert', 'tensor')), may hold values 0 or 1
- saved_gate: bfloat16 [64, 4, 8, 5, 1408], P(('expert', 'tensor'), None, None, None, 'dp'), may hold values from -6 to 6
- saved_up: bfloat16 [64, 4, 8, 5, 1408], P(('expert', 'tensor'), None, None, None, 'dp'), may hold values from -6 to 6
- w_gate: bfloat16 [64, 2048, 1408], P(('expert', 'tensor'), None, 'dp'), may hold values from -0.125 to 0.125
- w_up: bfloat16 [64, 2048, 1408], P(('expert', 'tensor'), None, 'dp'), may hold values from -0.125 to 0.125
- w_down: bfloat16 [64, 1408, 2048], P(('expert', 'tensor'), 'dp'), may hold values from -0.15625 to 0.15625
- shared_gate_act: bfloat16 [4096, 1408], P(('dp', 'expert'), 'tensor'), may hold values from -6 to 6
- shared_up_act: bfloat16 [4096, 1408], P(('dp', 'expert'), 'tensor'), may hold values from -6 to 6
- ws_gate: bfloat16 [2048, 1408], P(None, 'tensor'), may hold values from -0.125 to 0.125
- ws_up: bfloat16 [2048, 1408], P(None, 'tensor'), may hold values from -0.125 to 0.125
- ws_down: bfloat16 [1408, 2048], P('tensor'), may hold values from -0.15625 to 0.15625
- w_out: bfloat16 [2048, 2048], P('tensor'), may hold values from -0.125 to 0.125
Outputs:
- grad_hidden: bfloat16 [4096, 2048], P(('dp', 'expert', 'tensor'))
- grad_context: bfloat16 [4096, 2048], P(('dp', 'expert'), 'tensor')
Inputs may be any that keep to these rules, and one draw needn't show every extreme that they name: `expert_ids`: each row names 2 different experts; within the rows of one device (aligned blocks of 128 rows) no expert is named by more than 5 rows, a bound that some block reaches.
All inputs are finite; a program needn't handle non-finite values. No bound on the sum of `overflow` on one device may be relied on, other than what follows from the above.
Results may differ from a plain program's by a relative error of at most 0.015.
Values may be sent and summed in bfloat16 or wider, within the bound.
No kernel may reach another device: no remote copies, remote signals or barrier semaphores. Data moves between devices by JAX's collectives and lax.ppermute only.
A program may use at most 128 MiB of HBM per device.

v0:
```python
import jax
import jax.numpy as jnp
from jax import lax
from jax.sharding import PartitionSpec as P


def rank_in_block(pair_experts, expert_total):
    onehot = (pair_experts[:, None] == jnp.arange(expert_total, dtype=jnp.int32)[None, :]).astype(
        jnp.int32
    )
    earlier = jnp.cumsum(onehot, axis=0) - onehot
    return jnp.sum(earlier * onehot, axis=1)


def fill_slots(pair_grads, pair_experts, expert_total, capacity):
    pair_count, model_width = pair_grads.shape
    destination = pair_experts * capacity + rank_in_block(pair_experts, expert_total)
    source = jnp.full((expert_total * capacity,), pair_count, jnp.int32)
    source = source.at[destination].set(jnp.arange(pair_count, dtype=jnp.int32))
    padded = jnp.concatenate([pair_grads, jnp.zeros((1, model_width), pair_grads.dtype)], axis=0)
    return (padded[source].reshape(expert_total, capacity, model_width), destination)


def weighted_pairs(grads, weights):
    scaled = grads.astype(jnp.float32)[:, None, :] * weights.astype(jnp.float32)[:, :, None]
    return scaled.astype(jnp.bfloat16).reshape(-1, grads.shape[1])


def swiglu_backward(hidden_activation, gate_act, up_act):
    gate_value = gate_act.astype(jnp.float32)
    sigmoid_value = jax.nn.sigmoid(gate_value)
    gate_input_gradient = (
        hidden_activation
        * up_act.astype(jnp.float32)
        * sigmoid_value
        * (1.0 + gate_value * (1.0 - sigmoid_value))
    ).astype(jnp.bfloat16)
    up_input_gradient = (hidden_activation * gate_value * sigmoid_value).astype(jnp.bfloat16)
    return (gate_input_gradient, up_input_gradient)


def expert_terms(
    capacity_slot_rows,
    gate_act,
    up_act,
    gate_projection_weight,
    up_projection_weight,
    down_projection_weight,
):
    hidden_activation = jnp.einsum(
        "cyg,cog->cyo",
        capacity_slot_rows,
        down_projection_weight,
        preferred_element_type=jnp.float32,
    )
    gate_input_gradient, up_input_gradient = swiglu_backward(hidden_activation, gate_act, up_act)
    input_gradient_output = jnp.einsum(
        "etv,ebv->etb",
        gate_input_gradient,
        gate_projection_weight,
        preferred_element_type=jnp.float32,
    )
    input_gradient_output = input_gradient_output + jnp.einsum(
        "etv,ebv->etb", up_input_gradient, up_projection_weight, preferred_element_type=jnp.float32
    )
    return lax.optimization_barrier(input_gradient_output.astype(jnp.bfloat16))


def body(
    grad_out,
    expert_ids,
    gate_weights,
    overflow,
    saved_gate,
    saved_up,
    w_gate,
    w_up,
    w_down,
    shared_gate_act,
    shared_up_act,
    ws_gate,
    ws_up,
    ws_down,
    w_out,
):
    dp_count = lax.axis_size("dp")
    group_count = lax.axis_size(("expert", "tensor"))
    expert_local, unused_dp, unused_group, capacity, unit_part = saved_gate.shape
    expert_total = expert_local * group_count
    token_count, model_width = grad_out.shape
    top_count = expert_ids.shape[1]
    flag_values = overflow.astype(jnp.float32)
    routed_weight = (gate_weights * (1.0 - flag_values)).astype(jnp.bfloat16)
    shared_weight = 1.0 + jnp.sum(gate_weights * flag_values, axis=1)
    pair_grads = weighted_pairs(grad_out, routed_weight)
    filled, destination = fill_slots(pair_grads, expert_ids.reshape(-1), expert_total, capacity)
    arrived = lax.all_to_all(
        filled[:, None], ("expert", "tensor"), split_axis=0, concat_axis=1, tiled=True
    )
    everyone = lax.all_gather(arrived[:, None], "dp", axis=1, tiled=True)
    terms = expert_terms(
        everyone.reshape(expert_local, -1, model_width),
        saved_gate.reshape(expert_local, -1, unit_part),
        saved_up.reshape(expert_local, -1, unit_part),
        w_gate,
        w_up,
        w_down,
    )
    terms = terms.astype(jnp.float32).reshape(
        expert_local, dp_count, group_count, capacity, model_width
    )
    summed = lax.psum_scatter(
        terms.astype(jnp.bfloat16), "dp", scatter_dimension=1, tiled=True
    ).astype(jnp.float32)
    returned = lax.all_to_all(
        summed[:, 0].astype(jnp.bfloat16),
        ("expert", "tensor"),
        split_axis=1,
        concat_axis=0,
        tiled=True,
    ).astype(jnp.float32)
    picked = returned.reshape(expert_total * capacity, model_width)[destination]
    routed = jnp.sum(picked.reshape(token_count, top_count, model_width), axis=1)
    routed_total = routed.astype(jnp.bfloat16)
    shared_grad = (grad_out.astype(jnp.float32) * shared_weight[:, None]).astype(jnp.bfloat16)
    group_shared = lax.all_gather(shared_grad, "tensor", axis=0, tiled=True)
    shared_hidden = jnp.einsum(
        "td,fd->tf", group_shared, ws_down, preferred_element_type=jnp.float32
    )
    shared_gate_grad, shared_up_grad = swiglu_backward(
        shared_hidden, shared_gate_act, shared_up_act
    )
    partial_value = jnp.einsum(
        "tf,df->td", shared_gate_grad, ws_gate, preferred_element_type=jnp.float32
    )
    partial_value = partial_value + jnp.einsum(
        "tf,df->td", shared_up_grad, ws_up, preferred_element_type=jnp.float32
    )
    partial_value = lax.optimization_barrier(partial_value.astype(jnp.bfloat16)).astype(jnp.float32)
    own_shared = lax.psum_scatter(
        partial_value.astype(jnp.bfloat16), "tensor", scatter_dimension=0, tiled=True
    ).astype(jnp.float32)
    grad_hidden = (
        grad_out.astype(jnp.float32) + own_shared + routed_total.astype(jnp.float32)
    ).astype(jnp.bfloat16)
    grad_group = lax.all_gather(grad_hidden, "tensor", axis=0, tiled=True)
    grad_context = jnp.einsum(
        "td,hd->th", grad_group, w_out, preferred_element_type=jnp.float32
    ).astype(jnp.bfloat16)
    return (grad_hidden, grad_context)


def solution(mesh):
    in_specs = (
        P(("dp", "expert", "tensor"), None),
        P(("dp", "expert", "tensor"), None),
        P(("dp", "expert", "tensor"), None),
        P(("dp", "expert", "tensor"), None),
        P(("expert", "tensor"), None, None, None, "dp"),
        P(("expert", "tensor"), None, None, None, "dp"),
        P(("expert", "tensor"), None, "dp"),
        P(("expert", "tensor"), None, "dp"),
        P(("expert", "tensor"), "dp", None),
        P(("dp", "expert"), "tensor"),
        P(("dp", "expert"), "tensor"),
        P(None, "tensor"),
        P(None, "tensor"),
        P("tensor", None),
        P("tensor", None),
    )
    out_specs = (P(("dp", "expert", "tensor"), None), P(("dp", "expert"), "tensor"))
    return jax.shard_map(body, mesh=mesh, in_specs=in_specs, out_specs=out_specs, check_vma=False)
```

profile of v0, /device:TPU:0, one launch (start us, length us, event | category | flops | bytes accessed | tf_op | source)
XLA Modules:
  0.0 329.5 jit_solution(9769154388567705892)
XLA Ops:
  12.8 3.4 %mul.98 = f32[128,2,2048]{2,1,0:T(2,128)} broadcast(bf16[128,2048]{1,0:T(8,128)(2,1)} %param.15), dimensions={0,2} | broadcast | bytes 2621440 | tf_op jit(solution)/shard_map/mul | solution.py:25
  16.2 3.7 %mul.99 = f32[256,2048]{1,0:T(8,128)} reshape(f32[128,2,2048]{2,1,0:T(2,128)} %mul.98) | data formatting | bytes 4194304 | tf_op jit(solution)/shard_map/mul | solution.py:25
  22.7 6.3 %gather_fusion = bf16[320,2048]{1,0:T(8,128)(2,1)} fusion(bf16[257,2048]{1,0:T(8,128)(2,1)} %concatenate.3, s32[1024]{0:T(1024)S(1)} %pad_clamp_fusion.1), kind=kCustom, calls=%fused_computation | custom fusion | bytes 2622720 | tf_op jit(solution)/shard_map/gather | solution.py:21
  29.1 3.4 %broadcast_in_dim_reshape.4 = bf16[64,1,5,2048]{3,2,0,1:T(8,128)(2,1)} reshape(bf16[320,2048]{1,0:T(8,128)(2,1)} %gather_fusion) | data formatting | bytes 2621440 | tf_op jit(solution)/shard_map/broadcast_in_dim;reshape | solution.py:98
  32.5 55.5 %all_to_all.24 = bf16[64,1,5,2048]{3,2,1,0:T(8,128)(2,1)S(1)} all-to-all(bf16[64,1,5,2048]{3,2,1,0:T(8,128)(2,1)} %bitcast.53), channel_id=1, replica_groups=mesh['dp'=4,'expert'=4,'tensor'=2] {'expert','tensor'}, dimensions={0} | all-to-all | bytes 2621440 | tf_op jit(solution)/shard_map/all_to_all | solution.py:97
  96.5 33.0 %all-gather.9.cloned.1.call-done = bf16[8,32,1,5,2048]{4,0,1,3,2:T(8,128)(2,1)} async-done(((bf16[8,8,1,5,2048]{4,0,1,3,2:T(8,128)(2,1)}), bf16[8,32,1,5,2048]{4,0,1,3,2:T(8,128)(2,1)}) %all-gather.9.cloned.1.call-update) | async-done | bytes 5242896 | tf_op jit(solution)/shard_map/all_gather | solution.py:100
  129.6 5.7 %copy.43 = bf16[8,32,1,5,2048]{4,0,3,1,2:T(8,128)(2,1)} copy(bf16[8,32,1,5,2048]{4,0,1,3,2:T(8,128)(2,1)} %all-gather.9.cloned.1.call-done) | data formatting | bytes 10485760 | tf_op jit(solution)/shard_map/all_gather | solution.py:100
  135.3 15.0 %fusion = f32[8,160,352]{2,1,0:T(8,128)} fusion(bf16[8,352,2048]{2,1,0:T(8,128)(2,1)} %param.23, bf16[8,160,2048]{2,0,1:T(8,128)(2,1)} %bitcast.54), kind=kOutput, calls=%fused_computation.4 | convolution fusion | flops 1845493760 | bytes 18579456 | tf_op jit(solution)/shard_map/cyg,cog->cyo/dot_general | solution.py:50
  150.2 13.2 %fusion.6 = f32[8,160,2048]{2,1,0:T(8,128)} fusion(bf16[8,2048,352]{1,2,0:T(8,128)(2,1)} %param.21, f32[8,160,352]{2,1,0:T(8,128)} %fusion, f32[8,160,352]{2,0,1:T(8,128)} %bitcast_convert_fusion, f32[8,160,352]{2,0,1:T(8,128)S(1)} %copy-done.1), kind=kOutput, calls=%fused_computation.23 | convolution fusion | flops 1849999360 | bytes 27426816 | tf_op jit(solution)/shard_map/etv,ebv->etb/dot_general | solution.py:57
  163.4 13.3 %add_convert_fusion = bf16[8,160,2048]{2,1,0:T(8,128)(2,1)} fusion(f32[8,160,2048]{2,1,0:T(8,128)} %fusion.6, bf16[8,2048,352]{1,2,0:T(8,128)(2,1)} %param.22, f32[8,160,352]{2,1,0:T(8,128)} %fusion, f32[8,160,352]{2,0,1:T(8,128)S(1)} %copy-done.1), kind=kOutput, calls=%fused_computation.3 | convolution fusion | flops 1853440000 | bytes 30867456 | tf_op jit(solution)/shard_map/etv,ebv->etb/dot_general | solution.py:63
  176.8 7.7 %copy.51 = bf16[8,160,2048]{2,0,1:T(8,128)(2,1)} copy(bf16[8,160,2048]{2,1,0:T(8,128)(2,1)} %add_convert_fusion) | data formatting | bytes 10485760 | tf_op jit(solution)/shard_map/optimization_barrier | solution.py:66
  184.5 4.0 %fusion.34 = f32[256,704]{0,1:T(8,128)} fusion(bf16[256,2048]{1,0:T(8,128)(2,1)} %all-gather.5.cloned.1.call-done, bf16[704,2048]{1,0:T(8,128)(2,1)} %param.28), kind=kOutput, calls=%fused_computation.63 | convolution fusion | flops 738197504 | bytes 4653056 | tf_op jit(solution)/shard_map/td,fd->tf/dot_general | solution.py:127
  188.5 47.5 %reduce-scatter.5.cloned.1.call-done = bf16[8,1,8,5,2048]{4,0,3,2,1:T(8,128)(2,1)} async-done(((bf16[8,4,8,5,2048]{4,0,3,2,1:T(8,128)(2,1)}), bf16[8,1,8,5,2048]{4,0,3,2,1:T(8,128)(2,1)}) %reduce-scatter.5.cloned.1.call-update) | async-done | bytes 1310736 | tf_op jit(solution)/shard_map/reduce_scatter | solution.py:112
  236.0 5.5 %all-to-all-start.1 = ((bf16[8,8,5,2048]{3,0,2,1:T(8,128)(2,1)}), bf16[8,8,5,2048]{3,0,2,1:T(8,128)(2,1)}, u32[]{:S(2)}, u32[]{:S(2)}) async-start(bf16[8,8,5,2048]{3,0,2,1:T(8,128)(2,1)} %bitcast.56), calls=%async_computation.3 | async-start | bytes 2621440 | tf_op jit(solution)/shard_map/all_to_all | solution.py:115
  241.6 2.5 fusion.19
  246.4 26.4 %all-to-all-done.1 = bf16[8,8,5,2048]{3,0,2,1:T(8,128)(2,1)} async-done(((bf16[8,8,5,2048]{3,0,2,1:T(8,128)(2,1)}), bf16[8,8,5,2048]{3,0,2,1:T(8,128)(2,1)}, u32[]{:S(2)}, u32[]{:S(2)}) %all-to-all-start.1) | async-done | bytes 1310752 | tf_op jit(solution)/shard_map/all_to_all | solution.py:115
  274.4 3.5 %copy.52 = f32[8,8,1,5,2048]{4,3,1,0,2:T(8,128)} copy(f32[8,8,1,5,2048]{4,1,3,0,2:T(8,128)S(1)} %convert_bitcast_fusion) | data formatting | bytes 5242880 | tf_op jit(solution)/shard_map/convert_element_type | solution.py:121
  277.9 4.6 %reshape.91 = f32[320,2048]{1,0:T(8,128)} reshape(f32[8,8,1,5,2048]{4,3,1,0,2:T(8,128)} %copy.52) | data formatting | bytes 5242880 | tf_op jit(solution)/shard_map/convert_element_type | solution.py:121
  282.5 5.4 %gather_fusion.1 = f32[256,2048]{1,0:T(8,128)} fusion(f32[320,2048]{1,0:T(8,128)} %reshape.91, s32[1024]{0:T(1024)S(1)} %pad_clamp_fusion), kind=kCustom, calls=%fused_computation.1 | custom fusion | bytes 4195328 | tf_op jit(solution)/shard_map/gather | solution.py:122
  287.8 3.5 %reshape.87 = f32[128,2,2048]{2,1,0:T(2,128)} reshape(f32[256,2048]{1,0:T(8,128)} %gather_fusion.1) | data formatting | bytes 4194304 | tf_op jit(solution)/shard_map/reshape | solution.py:123
  291.3 5.0 %reduce_sum.32 = bf16[128,2048]{1,0:T(8,128)(2,1)} reduce(f32[128,2,2048]{2,1,0:T(2,128)} %reshape.87, f32[]{:T(128)} %constant.8.clone.1), dimensions={1}, to_apply=%region_7.8 | reduce | flops 262144 | bytes 2621444 | tf_op jit(solution)/shard_map/reduce_sum | solution.py:123
  296.3 2.2 add_convert_fusion.1
  298.6 19.6 %all-gather.7.cloned.1.call-done = bf16[256,2048]{1,0:T(8,128)(2,1)} async-done(((bf16[128,2048]{1,0:T(8,128)(2,1)}), bf16[256,2048]{1,0:T(8,128)(2,1)}) %all-gather.7.cloned.1.call-update) | async-done | bytes 1048592 | tf_op jit(solution)/shard_map/all_gather | solution.py:146
  318.2 4.6 %convolution_convert_fusion = bf16[256,1024]{1,0:T(8,128)(2,1)} fusion(bf16[256,2048]{1,0:T(8,128)(2,1)} %all-gather.7.cloned.1.call-done, bf16[1024,2048]{1,0:T(8,128)(2,1)} %param.29), kind=kOutput, calls=%fused_computation.17 | convolution fusion | flops 1074003968 | bytes 5767168 | tf_op jit(solution)/shard_map/td,hd->th/dot_general | solution.py:147
  (60 shorter events, 20.9 us)
Async XLA Ops:
  7.2 234.4 %copy-start = (bf16[2048,704]{0,1:T(8,128)(2,1)S(1)}, bf16[2048,704]{0,1:T(8,128)(2,1)}, u32[]{:S(2)}) copy-start(bf16[2048,704]{0,1:T(8,128)(2,1)} %param.26) | copy-start | bytes 8650756
  7.2 122.4 %all-gather.9.cloned.1.call-start = ((), (), s32[]{:S(2)}) async-start(), calls=%async_computation.8 | async-start | bytes 6553600 | tf_op jit(solution)/shard_map/all_gather | solution.py:100
  88.0 2.1 copy-start.2
  90.0 94.5 %all-gather.5.cloned.1.call-start = ((), (), s32[]{:S(2)}) async-start(), calls=%async_computation.4 | async-start | bytes 1572864 | tf_op jit(solution)/shard_map/all_gather | solution.py:126
  91.0 145.0 %reduce-scatter.5.cloned.1.call-start = ((), (), s32[]{:S(2)}) async-start(), calls=%async_computation.6 | async-start | bytes 6553600 | tf_op jit(solution)/shard_map/reduce_scatter | solution.py:112
  91.5 3.2 copy-start.5
  135.3 15.0 %copy-start.1 = (f32[8,160,352]{2,0,1:T(8,128)S(1)}, f32[8,160,352]{2,0,1:T(8,128)}, u32[]{:S(2)}) copy-start(f32[8,160,352]{2,0,1:T(8,128)} %bitcast_convert_fusion.1) | copy-start | bytes 5406724
  188.5 53.1 %copy-start.7 = (bf16[256,704]{0,1:T(8,128)(2,1)S(1)}, bf16[256,704]{0,1:T(8,128)(2,1)}, u32[]{:S(2)}) copy-start(bf16[256,704]{0,1:T(8,128)(2,1)} %param.24) | copy-start | bytes 1081348
  236.0 36.8 %all-to-all-start.1 = ((bf16[8,8,5,2048]{3,0,2,1:T(8,128)(2,1)}), bf16[8,8,5,2048]{3,0,2,1:T(8,128)(2,1)}, u32[]{:S(2)}, u32[]{:S(2)}) async-start(bf16[8,8,5,2048]{3,0,2,1:T(8,128)(2,1)} %bitcast.56), calls=%async_computation.3 | async-start | bytes 2621440 | tf_op jit(solution)/shard_map/all_to_all | solution.py:115
  241.5 54.8 %reduce-scatter.3.cloned.1.call-start = ((), (), s32[]{:S(2)}) async-start(), calls=%async_computation.5 | async-start | bytes 1572864 | tf_op jit(solution)/shard_map/reduce_scatter | solution.py:140
  241.5 2.5 copy-start.4
  241.6 2.5 copy-start.6
  246.1 72.0 %all-gather.7.cloned.1.call-start = ((), (), s32[]{:S(2)}) async-start(), calls=%async_computation.7 | async-start | bytes 1572864 | tf_op jit(solution)/shard_map/all_gather | solution.py:146
  291.3 5.0 %copy-start.3 = (bf16[128,2048]{1,0:T(8,128)(2,1)S(1)}, bf16[128,2048]{1,0:T(8,128)(2,1)}, u32[]{:S(2)}) copy-start(bf16[128,2048]{1,0:T(8,128)(2,1)} %param.15) | copy-start | bytes 1572868
Sparse Core Ops, SparseCore 0:
  90.1 39.4 all-gather.8
  131.7 21.2 all-gather.4
  184.6 51.3 reduce-scatter.4
  246.3 26.1 reduce-scatter.2
  298.7 19.4 all-gather.6
where the time goes:
time: 336 us; the launch traced here: 330 us
  waiting for transfers between devices  127 us (38%)
  blocking collectives  55.5 us (17%)
  local copies, waits for them, and re-layouts  55.4 us (16%)
  matrix products  54.6 us (16%)
  other arithmetic  16.8 us (5%)
  between operations  14.2 us (4%)
  starting transfers between devices  6.39 us (2%)
    all_to_all x1, blocking collectives, body(): lax.all_to_all(filled[:, None], ('expert', 'tensor'), split_axis=0, conca...  55.5 us
    reduce_scatter x1, waiting for transfers between devices, body(): lax.psum_scatter(terms.astype(jnp.bfloat16), 'dp', scatter_dimension=1, t...  47.5 us
    all_gather x1, waiting for transfers between devices, body(): everyone = lax.all_gather(arrived[:, None], 'dp', axis=1, tiled=True)  33 us
    all_to_all x1, waiting for transfers between devices, body(): lax.all_to_all(summed[:, 0].astype(jnp.bfloat16), ('expert', 'tensor'), s...  26.4 us
    all_gather x1, waiting for transfers between devices, body(): grad_group = lax.all_gather(grad_hidden, 'tensor', axis=0, tiled=True)  19.6 us
    dot_general x1, matrix products, expert_terms(): jnp.einsum('cyg,cog->cyo', capacity_slot_rows, down_projection_weight, pr...  15 us
    dot_general x1, matrix products, expert_terms(): jnp.einsum('etv,ebv->etb', up_input_gradient, up_projection_weight, prefe...  13.3 us
    dot_general x1, matrix products, expert_terms(): jnp.einsum('etv,ebv->etb', gate_input_gradient, gate_projection_weight, p...  13.2 us
  transfers between devices with their start and end apart: 6, of which 4 were waited for; matrix products, arithmetic and copies ran while one was open for 28% of the time, Pallas kernels for 0%

commit v1 on v0

--- a/solution.py
+++ b/solution.py
@@ -2,6 +2,25 @@
 import jax.numpy as jnp
 from jax import lax
 from jax.sharding import PartitionSpec as P
+
+
+def laid_out(tiles, dim):
+    tiles = jnp.moveaxis(tiles, 0, dim)
+    dims = tiles.shape
+    return tiles.reshape(*dims[:dim], dims[dim] * dims[dim + 1], *dims[dim + 2 :])
+
+
+def ring_apply(shard, axis, dim, work, out_dim):
+    devices, position, span = (lax.axis_size(axis), lax.axis_index(axis), shard.shape[dim])
+    upward = [(i, (i + 1) % devices) for i in range(devices)]
+    blocks = []
+    held = shard
+    for step in range(devices):
+        arriving = held if step == devices - 1 else lax.ppermute(held, axis, upward)
+        blocks.append(work(held, (position - step) % devices * span))
+        held = arriving
+    blocks = jnp.stack(blocks)[(position - jnp.arange(devices)) % devices]
+    return laid_out(blocks, out_dim)
 
 
 def rank_in_block(pair_experts, expert_total):
@@ -143,9 +162,14 @@
     grad_hidden = (
         grad_out.astype(jnp.float32) + own_shared + routed_total.astype(jnp.float32)
     ).astype(jnp.bfloat16)
-    grad_group = lax.all_gather(grad_hidden, "tensor", axis=0, tiled=True)
-    grad_context = jnp.einsum(
-        "td,hd->th", grad_group, w_out, preferred_element_type=jnp.float32
+    grad_context = ring_apply(
+        grad_hidden,
+        "tensor",
+        0,
+        lambda shard, offset: jnp.einsum(
+            "td,hd->th", shard, w_out, preferred_element_type=jnp.float32
+        ),
+        0,
     ).astype(jnp.bfloat16)
     return (grad_hidden, grad_context)
 

time: 336 us -> 326 us (0.970)
  waiting for transfers between devices: 127 us -> 114 us
    all_gather x1 -> x0, waiting for transfers between devices: 19.6 us -> none  [body(): grad_group = lax.all_gather(grad_hidden, 'tensor', axis=0, tiled=True)]
    ppermute x0 -> x1, waiting for transfers between devices: none -> 7.26 us  [ring_apply(): arriving = held if step == devices - 1 else lax.ppermute(held, axis, upward)]
  transfers between devices with their start and end apart: 6 -> 6, of which waited for: 4 -> 4; matrix products, arithmetic and copies ran while one was open for 28% -> 30% of each run, Pallas kernels for 0% -> 0%
where the time goes in v1:
time: 326 us; the launch traced here: 320 us
  waiting for transfers between devices  114 us (35%)
  local copies, waits for them, and re-layouts  56.8 us (17%)
  blocking collectives  55.5 us (17%)
  matrix products  55.4 us (17%)
  other arithmetic  16.1 us (5%)
  between operations  14.2 us (4%)
  starting transfers between devices  7.87 us (2%)
    all_to_all x1, blocking collectives, body(): lax.all_to_all(filled[:, None], ('expert', 'tensor'), split_axis=0, conca...  55.5 us
    reduce_scatter x1, waiting for transfers between devices, body(): lax.psum_scatter(terms.astype(jnp.bfloat16), 'dp', scatter_dimension=1, t...  47.5 us
    all_gather x1, waiting for transfers between devices, body(): everyone = lax.all_gather(arrived[:, None], 'dp', axis=1, tiled=True)  33 us
    all_to_all x1, waiting for transfers between devices, body(): lax.all_to_all(summed[:, 0].astype(jnp.bfloat16), ('expert', 'tensor'), s...  26.4 us
    dot_general x1, matrix products, expert_terms(): jnp.einsum('cyg,cog->cyo', capacity_slot_rows, down_projection_weight, pr...  15 us
    dot_general x1, matrix products, expert_terms(): jnp.einsum('etv,ebv->etb', up_input_gradient, up_projection_weight, prefe...  13.3 us
    dot_general x1, matrix products, expert_terms(): jnp.einsum('etv,ebv->etb', gate_input_gradient, gate_projection_weight, p...  13.2 us
    convert_element_type x2, local copies, waits for them, and re-layouts, body(): returned = lax.all_to_all(summed[:, 0].astype(jnp.bfloat16), ('expert', '...  8.05 us
  transfers between devices with their start and end apart: 6, of which 4 were waited for; matrix products, arithmetic and copies ran while one was open for 30% of the time, Pallas kernels for 0%

profile of v1, /device:TPU:0, one launch (start us, length us, event | category | flops | bytes accessed | tf_op | source)
XLA Modules:
  0.0 320.2 jit_solution(1572355414896496289)
XLA Ops:
  12.8 3.4 %mul.98 = f32[128,2,2048]{2,1,0:T(2,128)} broadcast(bf16[128,2048]{1,0:T(8,128)(2,1)} %param.15), dimensions={0,2} | broadcast | bytes 2621440 | tf_op jit(solution)/shard_map/mul | solution.py:44
  16.2 3.7 %mul.99 = f32[256,2048]{1,0:T(8,128)} reshape(f32[128,2,2048]{2,1,0:T(2,128)} %mul.98) | data formatting | bytes 4194304 | tf_op jit(solution)/shard_map/mul | solution.py:44
  22.7 6.3 %gather_fusion = bf16[320,2048]{1,0:T(8,128)(2,1)} fusion(bf16[257,2048]{1,0:T(8,128)(2,1)} %concatenate.3, s32[1024]{0:T(1024)S(1)} %pad_clamp_fusion.2), kind=kCustom, calls=%fused_computation | custom fusion | bytes 2622720 | tf_op jit(solution)/shard_map/gather | solution.py:40
  29.1 3.4 %broadcast_in_dim_reshape.4 = bf16[64,1,5,2048]{3,2,0,1:T(8,128)(2,1)} reshape(bf16[320,2048]{1,0:T(8,128)(2,1)} %gather_fusion) | data formatting | bytes 2621440 | tf_op jit(solution)/shard_map/broadcast_in_dim;reshape | solution.py:117
  32.5 55.5 %all_to_all.24 = bf16[64,1,5,2048]{3,2,1,0:T(8,128)(2,1)S(1)} all-to-all(bf16[64,1,5,2048]{3,2,1,0:T(8,128)(2,1)} %bitcast.62), channel_id=1, replica_groups=mesh['dp'=4,'expert'=4,'tensor'=2] {'expert','tensor'}, dimensions={0} | all-to-all | bytes 2621440 | tf_op jit(solution)/shard_map/all_to_all | solution.py:116
  96.5 33.0 %all-gather.6.cloned.1.call-done = bf16[8,32,1,5,2048]{4,0,1,3,2:T(8,128)(2,1)} async-done(((bf16[8,8,1,5,2048]{4,0,1,3,2:T(8,128)(2,1)}), bf16[8,32,1,5,2048]{4,0,1,3,2:T(8,128)(2,1)}) %all-gather.6.cloned.1.call-update) | async-done | bytes 5242896 | tf_op jit(solution)/shard_map/all_gather | solution.py:119
  129.6 5.7 %copy.43 = bf16[8,32,1,5,2048]{4,0,3,1,2:T(8,128)(2,1)} copy(bf16[8,32,1,5,2048]{4,0,1,3,2:T(8,128)(2,1)} %all-gather.6.cloned.1.call-done) | data formatting | bytes 10485760 | tf_op jit(solution)/shard_map/all_gather | solution.py:119
  135.3 15.0 %fusion = f32[8,160,352]{2,1,0:T(8,128)} fusion(bf16[8,352,2048]{2,1,0:T(8,128)(2,1)} %param.23, bf16[8,160,2048]{2,0,1:T(8,128)(2,1)} %bitcast.63), kind=kOutput, calls=%fused_computation.5 | convolution fusion | flops 1845493760 | bytes 18579456 | tf_op jit(solution)/shard_map/cyg,cog->cyo/dot_general | solution.py:69
  150.2 13.2 %fusion.6 = f32[8,160,2048]{2,1,0:T(8,128)} fusion(bf16[8,2048,352]{1,2,0:T(8,128)(2,1)} %param.21, f32[8,160,352]{2,1,0:T(8,128)} %fusion, f32[8,160,352]{2,0,1:T(8,128)} %bitcast_convert_fusion, f32[8,160,352]{2,0,1:T(8,128)S(1)} %copy-done.1), kind=kOutput, calls=%fused_computation.26 | convolution fusion | flops 1849999360 | bytes 27426816 | tf_op jit(solution)/shard_map/etv,ebv->etb/dot_general | solution.py:76
  163.4 13.3 %add_convert_fusion = bf16[8,160,2048]{2,1,0:T(8,128)(2,1)} fusion(f32[8,160,2048]{2,1,0:T(8,128)} %fusion.6, bf16[8,2048,352]{1,2,0:T(8,128)(2,1)} %param.22, f32[8,160,352]{2,1,0:T(8,128)} %fusion, f32[8,160,352]{2,0,1:T(8,128)S(1)} %copy-done.1), kind=kOutput, calls=%fused_computation.4 | convolution fusion | flops 1853440000 | bytes 30867456 | tf_op jit(solution)/shard_map/etv,ebv->etb/dot_general | solution.py:82
  176.8 7.7 %copy.51 = bf16[8,160,2048]{2,0,1:T(8,128)(2,1)} copy(bf16[8,160,2048]{2,1,0:T(8,128)(2,1)} %add_convert_fusion) | data formatting | bytes 10485760 | tf_op jit(solution)/shard_map/optimization_barrier | solution.py:85
  184.5 4.0 %fusion.36 = f32[256,704]{0,1:T(8,128)} fusion(bf16[256,2048]{1,0:T(8,128)(2,1)} %all-gather.4.cloned.1.call-done, bf16[704,2048]{1,0:T(8,128)(2,1)} %param.28), kind=kOutput, calls=%fused_computation.73 | convolution fusion | flops 738197504 | bytes 4653056 | tf_op jit(solution)/shard_map/td,fd->tf/dot_general | solution.py:146
  188.5 47.5 %reduce-scatter.5.cloned.1.call-done = bf16[8,1,8,5,2048]{4,0,3,2,1:T(8,128)(2,1)} async-done(((bf16[8,4,8,5,2048]{4,0,3,2,1:T(8,128)(2,1)}), bf16[8,1,8,5,2048]{4,0,3,2,1:T(8,128)(2,1)}) %reduce-scatter.5.cloned.1.call-update) | async-done | bytes 1310736 | tf_op jit(solution)/shard_map/reduce_scatter | solution.py:131
  236.0 5.5 %all-to-all-start.1 = ((bf16[8,8,5,2048]{3,0,2,1:T(8,128)(2,1)}), bf16[8,8,5,2048]{3,0,2,1:T(8,128)(2,1)}, u32[]{:S(2)}, u32[]{:S(2)}) async-start(bf16[8,8,5,2048]{3,0,2,1:T(8,128)(2,1)} %bitcast.65), calls=%async_computation.3 | async-start | bytes 2621440 | tf_op jit(solution)/shard_map/all_to_all | solution.py:134
  241.8 2.5 fusion.19
  244.3 2.0 fusion.2
  246.4 26.4 %all-to-all-done.1 = bf16[8,8,5,2048]{3,0,2,1:T(8,128)(2,1)} async-done(((bf16[8,8,5,2048]{3,0,2,1:T(8,128)(2,1)}), bf16[8,8,5,2048]{3,0,2,1:T(8,128)(2,1)}, u32[]{:S(2)}, u32[]{:S(2)}) %all-to-all-start.1) | async-done | bytes 1310752 | tf_op jit(solution)/shard_map/all_to_all | solution.py:134
  274.4 3.5 %copy.52 = f32[8,8,1,5,2048]{4,3,1,0,2:T(8,128)} copy(f32[8,8,1,5,2048]{4,1,3,0,2:T(8,128)S(1)} %convert_bitcast_fusion) | data formatting | bytes 5242880 | tf_op jit(solution)/shard_map/convert_element_type | solution.py:140
  277.9 4.6 %reshape.142 = f32[320,2048]{1,0:T(8,128)} reshape(f32[8,8,1,5,2048]{4,3,1,0,2:T(8,128)} %copy.52) | data formatting | bytes 5242880 | tf_op jit(solution)/shard_map/convert_element_type | solution.py:140
  282.5 5.4 %gather_fusion.1 = f32[256,2048]{1,0:T(8,128)} fusion(f32[320,2048]{1,0:T(8,128)} %reshape.142, s32[1024]{0:T(1024)S(1)} %pad_clamp_fusion.1), kind=kCustom, calls=%fused_computation.1 | custom fusion | bytes 4195328 | tf_op jit(solution)/shard_map/gather | solution.py:141
  287.8 3.5 %reshape.138 = f32[128,2,2048]{2,1,0:T(2,128)} reshape(f32[256,2048]{1,0:T(8,128)} %gather_fusion.1) | data formatting | bytes 4194304 | tf_op jit(solution)/shard_map/reshape | solution.py:142
  291.3 5.0 %reduce_sum.32 = bf16[128,2048]{1,0:T(8,128)(2,1)} reduce(f32[128,2,2048]{2,1,0:T(2,128)} %reshape.138, f32[]{:T(128)} %constant.12.clone.1), dimensions={1}, to_apply=%region_7.8 | reduce | flops 262144 | bytes 2621444 | tf_op jit(solution)/shard_map/reduce_sum | solution.py:142
  299.3 3.9 %convolution_bitcast_fusion.1 = bf16[1,128,1024]{2,1,0:T(8,128)(2,1)S(1)} fusion(bf16[128,2048]{1,0:T(8,128)(2,1)S(1)} %add_convert_fusion.1, bf16[1024,2048]{1,0:T(8,128)(2,1)} %param.29), kind=kOutput, calls=%fused_computation.19 | convolution fusion | flops 536870912 | bytes 4980736 | tf_op jit(solution)/shard_map/td,hd->th/dot_general | solution.py:169
  303.3 7.3 %collective-permute-done = bf16[128,2048]{1,0:T(8,128)(2,1)S(1)} collective-permute-done((bf16[128,2048]{1,0:T(8,128)(2,1)S(1)}, bf16[128,2048]{1,0:T(8,128)(2,1)S(1)}, u32[]{:S(2)}, u32[]{:S(2)}) %collective-permute-start) | collective-permute-done | bytes 524320 | tf_op jit(solution)/shard_map/ppermute | solution.py:19
  (68 shorter events, 24.7 us)
Async XLA Ops:
  7.2 234.6 %copy-start = (bf16[2048,704]{0,1:T(8,128)(2,1)S(1)}, bf16[2048,704]{0,1:T(8,128)(2,1)}, u32[]{:S(2)}) copy-start(bf16[2048,704]{0,1:T(8,128)(2,1)} %param.26) | copy-start | bytes 8650756
  7.2 122.4 %all-gather.6.cloned.1.call-start = ((), (), s32[]{:S(2)}) async-start(), calls=%async_computation.7 | async-start | bytes 6553600 | tf_op jit(solution)/shard_map/all_gather | solution.py:119
  88.0 2.1 copy-start.3
  90.0 94.5 %all-gather.4.cloned.1.call-start = ((), (), s32[]{:S(2)}) async-start(), calls=%async_computation.4 | async-start | bytes 1572864 | tf_op jit(solution)/shard_map/all_gather | solution.py:145
  91.0 145.0 %reduce-scatter.5.cloned.1.call-start = ((), (), s32[]{:S(2)}) async-start(), calls=%async_computation.6 | async-start | bytes 6553600 | tf_op jit(solution)/shard_map/reduce_scatter | solution.py:131
  91.5 3.2 copy-start.7
  135.3 15.0 %copy-start.1 = (f32[8,160,352]{2,0,1:T(8,128)S(1)}, f32[8,160,352]{2,0,1:T(8,128)}, u32[]{:S(2)}) copy-start(f32[8,160,352]{2,0,1:T(8,128)} %bitcast_convert_fusion.1) | copy-start | bytes 5406724
  188.5 53.3 %copy-start.9 = (bf16[256,704]{0,1:T(8,128)(2,1)S(1)}, bf16[256,704]{0,1:T(8,128)(2,1)}, u32[]{:S(2)}) copy-start(bf16[256,704]{0,1:T(8,128)(2,1)} %param.24) | copy-start | bytes 1081348
  236.0 36.8 %all-to-all-start.1 = ((bf16[8,8,5,2048]{3,0,2,1:T(8,128)(2,1)}), bf16[8,8,5,2048]{3,0,2,1:T(8,128)(2,1)}, u32[]{:S(2)}, u32[]{:S(2)}) async-start(bf16[8,8,5,2048]{3,0,2,1:T(8,128)(2,1)} %bitcast.65), calls=%async_computation.3 | async-start | bytes 2621440 | tf_op jit(solution)/shard_map/all_to_all | solution.py:134
  241.5 54.8 %reduce-scatter.3.cloned.1.call-start = ((), (), s32[]{:S(2)}) async-start(), calls=%async_computation.5 | async-start | bytes 1572864 | tf_op jit(solution)/shard_map/reduce_scatter | solution.py:159
  241.8 2.5 copy-start.5
  241.8 2.5 copy-start.8
  291.3 5.0 %copy-start.4 = (bf16[128,2048]{1,0:T(8,128)(2,1)S(1)}, bf16[128,2048]{1,0:T(8,128)(2,1)}, u32[]{:S(2)}) copy-start(bf16[128,2048]{1,0:T(8,128)(2,1)} %param.15) | copy-start | bytes 1572868
  297.8 5.5 %copy-start.6 = (bf16[128,2048]{1,0:T(8,128)(2,1)}, bf16[128,2048]{1,0:T(8,128)(2,1)S(1)}, u32[]{:S(2)}) copy-start(bf16[128,2048]{1,0:T(8,128)(2,1)S(1)} %add_convert_fusion.1) | copy-start | bytes 1572868
  297.8 12.7 %collective-permute-start = (bf16[128,2048]{1,0:T(8,128)(2,1)S(1)}, bf16[128,2048]{1,0:T(8,128)(2,1)S(1)}, u32[]{:S(2)}, u32[]{:S(2)}) collective-permute-start(bf16[128,2048]{1,0:T(8,128)(2,1)S(1)} %add_convert_fusion.1), channel_id=1, source_target_pairs={{0,1},{1,0},{2,3},{3,2},{4,5},{5,4},{6,7},{7,6},{8,9},{9,8},{10,11... | collective-permute-start | bytes 1572872 | tf_op jit(solution)/shard_map/ppermute | solution.py:19
  299.3 11.2 %copy-start.2 = (bf16[1024,2048]{1,0:T(8,128)(2,1)S(1)}, bf16[1024,2048]{1,0:T(8,128)(2,1)}, u32[]{:S(2)}) copy-start(bf16[1024,2048]{1,0:T(8,128)(2,1)} %param.29) | copy-start | bytes 12582916
Sparse Core Ops, SparseCore 0:
  90.1 39.4 all-gather.5
  131.7 21.2 all-gather.3
  184.6 51.3 reduce-scatter.4
  246.5 26.0 reduce-scatter.2
